TPU v7x, 32 devices: a whole 2x2x4 slice. The times are simulated.
32 devices in a mesh: ctx: 16 (over z, y, x), exp: 2 (over core).
Axes of the slice: x: 2, y: 2, z: 4, core: 2. Of those that a mesh axis runs over, the one named last changes fastest.
Arguments:
- attn_query: bfloat16 [2048, 4096], P('ctx', 'exp'), may hold values from -3 to 3
- attn_key: bfloat16 [2048, 4096], P('ctx', 'exp'), may hold values from -3 to 3
- attn_value: bfloat16 [2048, 4096], P('ctx', 'exp'), may hold values from -6 to 6
- log_decay: float32 [32, 2048], P('exp', 'ctx'), may hold values from -1 to 0
- cotangent: bfloat16 [2048, 4096], P('ctx', 'exp'), may hold values from -6 to 6
- expert_input: bfloat16 [2048, 4096], P('ctx', 'exp'), may hold values from -6 to 6
- router_gates: bfloat16 [2048, 4], P('ctx'), may hold values from 0.049804688 to 0.59765625
- expert_ids: int32 [2048, 4], P('ctx'), may hold values from 0 to 15, all different within a row; in each aligned block of 128 rows (0 to 127, 128 to 255, ...) at most 40 rows name the same one
- up_weights: bfloat16 [16, 4096, 1536], P('ctx', 'exp'), may hold values from -0.09375 to 0.09375
- down_weights: bfloat16 [16, 1536, 4096], P('ctx', None, 'exp'), may hold values from -0.15625 to 0.15625
Outputs:
- query_grad: bfloat16 [2048, 4096], P('ctx', 'exp')
- key_grad: bfloat16 [2048, 4096], P('ctx', 'exp')
- value_grad: bfloat16 [2048, 4096], P('ctx', 'exp')
- input_grad: bfloat16 [2048, 4096], P('ctx', 'exp')
- gate_grad: bfloat16 [2048, 4], P('ctx')
Inputs may be any that keep to these rules, and one draw needn't show every extreme that they name: `expert_ids`: each row names 4 different experts. Within the rows of one device (each aligned block of 128 rows) no expert is named more than 40 times, a bound that some block reaches.
All inputs are finite; a program needn't handle non-finite values.
Results may differ from a plain program's by a relative error of at most 0.025.
Values may be sent and summed in bfloat16 or wider, within the bound.
No kernel may reach another device: no remote copies, remote signals or barrier semaphores. Data moves between devices by JAX's collectives and lax.ppermute only.
A program may use at most 128 MiB of HBM per device.

v0:
```python
import jax
import jax.numpy as jnp
from jax import lax
from jax.sharding import PartitionSpec as P


def prefix(value, axis, join, neutral, backward):
    count = lax.axis_size(axis)
    place = lax.axis_index(axis)
    ahead = count - 1 - place if backward else place
    gathered = jax.tree.map(
        lambda a, kind: lax.all_gather(a.astype(kind), axis), value, (jnp.bfloat16, jnp.bfloat16)
    )
    state = jax.tree.map(lambda a, e: jnp.zeros_like(a) + jnp.asarray(e, a.dtype), value, neutral)

    def one(step, state):
        source = count - 1 - step if backward else step
        return join(
            state,
            jax.tree.map(
                lambda a, own: lax.dynamic_index_in_dim(a, source, 0, False).astype(own.dtype),
                gathered,
                value,
            ),
        )

    return lax.fori_loop(0, ahead, one, state)


def silu_slope(pre_act):
    sigmoid_val = jax.nn.sigmoid(pre_act)
    return sigmoid_val * (1.0 + pre_act * (1.0 - sigmoid_val))


def chain_step(earlier, later):
    return (earlier[0] + later[0], jnp.exp(later[0])[:, None, None] * earlier[1] + later[1])


def attention_part(attn_query, attn_key, attn_value, log_decay, cotangent):
    length, features = attn_query.shape
    head_count = log_decay.shape[0]
    head_size = features // head_count
    head_shape = (length, head_count, head_size)
    query_heads = attn_query.reshape(head_shape)
    key_head_rows = attn_key.reshape(head_shape)
    value_head_rows = attn_value.reshape(head_shape)
    cotangent_heads = cotangent.reshape(head_shape)
    cumul = jnp.cumsum(log_decay, axis=1)
    block_gain = cumul[:, -1]
    head_gain = jnp.exp(cumul).T[:, :, None]
    tail_gain = jnp.exp(block_gain[:, None] - cumul).T[:, :, None]
    scaled_key_rows = (tail_gain * key_head_rows).astype(jnp.bfloat16)
    scaled_query_rows = (head_gain * query_heads).astype(jnp.bfloat16)
    local_state = jnp.einsum(
        "qcb,qce->cbe", scaled_key_rows, value_head_rows, preferred_element_type=jnp.float32
    )
    local_adjoint = jnp.einsum(
        "iuo,iuf->uof", scaled_query_rows, cotangent_heads, preferred_element_type=jnp.float32
    )
    identity = (
        jnp.zeros((head_count,), jnp.float32),
        jnp.zeros((head_count, head_size, head_size), jnp.float32),
    )
    state_in = prefix((block_gain, local_state), "ctx", chain_step, identity, False)
    adjoint_in = prefix((block_gain, local_adjoint), "ctx", chain_step, identity, True)
    state_bfloat_copy = state_in[1].astype(jnp.bfloat16)
    adjoint_bfloat_copy = adjoint_in[1].astype(jnp.bfloat16)
    row_index = lax.broadcasted_iota(jnp.int32, (length, length), 0)
    col_index = lax.broadcasted_iota(jnp.int32, (length, length), 1)
    causal = (row_index >= col_index)[None, :, :]
    spread = cumul[:, :, None] - cumul[:, None, :]
    decay_mask = jnp.where(causal, jnp.exp(jnp.where(causal, spread, 0.0)), 0.0)
    cross_terms = jnp.einsum(
        "thv,shv->hts", cotangent_heads, value_head_rows, preferred_element_type=jnp.float32
    )
    scores = jnp.einsum(
        "thk,shk->hts", query_heads, key_head_rows, preferred_element_type=jnp.float32
    )
    cross_weights = (cross_terms * decay_mask).astype(jnp.bfloat16)
    score_weights = (scores * decay_mask).astype(jnp.bfloat16)
    query_part = jnp.einsum(
        "hts,shk->thk", cross_weights, key_head_rows, preferred_element_type=jnp.float32
    )
    query_part = query_part + head_gain * jnp.einsum(
        "gmi,mli->gml", cotangent_heads, state_bfloat_copy, preferred_element_type=jnp.float32
    )
    key_part = jnp.einsum(
        "hts,thk->shk", cross_weights, query_heads, preferred_element_type=jnp.float32
    )
    key_part = key_part + tail_gain * jnp.einsum(
        "ecf,cpf->ecp", value_head_rows, adjoint_bfloat_copy, preferred_element_type=jnp.float32
    )
    value_part = jnp.einsum(
        "hts,thv->shv", score_weights, cotangent_heads, preferred_element_type=jnp.float32
    )
    value_part = value_part + tail_gain * jnp.einsum(
        "owr,wru->owu", key_head_rows, adjoint_bfloat_copy, preferred_element_type=jnp.float32
    )
    scale = 1.0 / head_size
    query_grad = (query_part * scale).reshape(length, features).astype(jnp.bfloat16)
    key_grad = (key_part * scale).reshape(length, features).astype(jnp.bfloat16)
    value_grad = (value_part * scale).reshape(length, features).astype(jnp.bfloat16)
    return (query_grad, key_grad, value_grad)


def expert_part(cotangent, expert_input, router_gates, expert_ids, up_weights, down_weights):
    tokens, feature_share = expert_input.shape
    top_count = expert_ids.shape[1]
    experts = lax.axis_size("ctx")
    capacity = 5 * tokens * top_count // (4 * experts)
    flat_ids = expert_ids.reshape(-1)
    onehot = (flat_ids[:, None] == jnp.arange(experts, dtype=jnp.int32)[None, :]).astype(jnp.int32)
    before = jnp.cumsum(onehot, axis=0) - onehot
    slot_index = jnp.sum(before * onehot, axis=1)
    target = (flat_ids * capacity + slot_index).reshape(tokens, top_count)
    placed = target[None, :, :] == jnp.arange(experts * capacity, dtype=jnp.int32)[:, None, None]
    placed_float = placed.astype(jnp.float32)
    dispatch_rows = jnp.sum(placed_float, axis=2).astype(jnp.bfloat16)
    buffer_in = jnp.dot(dispatch_rows, expert_input, preferred_element_type=jnp.float32).astype(
        jnp.bfloat16
    )
    buffer_cot = jnp.dot(dispatch_rows, cotangent, preferred_element_type=jnp.float32).astype(
        jnp.bfloat16
    )
    buffer_gate = jnp.einsum("jtk,tk->j", placed_float, router_gates.astype(jnp.float32)).astype(
        jnp.bfloat16
    )
    buffer_in = buffer_in.reshape(experts, capacity, feature_share)
    buffer_cot = buffer_cot.reshape(experts, capacity, feature_share)
    buffer_gate = buffer_gate.reshape(experts, capacity)
    up_local = up_weights[0]
    down_local = down_weights[0]
    inputs = lax.all_to_all(buffer_in, "ctx", split_axis=0, concat_axis=0, tiled=True)
    cot_rows = lax.all_to_all(buffer_cot, "ctx", split_axis=0, concat_axis=0, tiled=True)
    gate_rows = lax.all_to_all(buffer_gate, "ctx", split_axis=0, concat_axis=0, tiled=True)
    sources, item_count, share_width = inputs.shape
    flat_in = inputs.reshape(sources * item_count, share_width)
    flat_cot = cot_rows.reshape(sources * item_count, share_width)
    gate_col = gate_rows.reshape(-1).astype(jnp.float32)
    part_pre = jnp.dot(flat_in, up_local, preferred_element_type=jnp.float32)
    part_back = lax.dot_general(
        flat_cot, down_local, (((1,), (1,)), ((), ())), preferred_element_type=jnp.float32
    )
    pre_act = lax.psum(part_pre.astype(jnp.bfloat16), "exp").astype(jnp.float32)
    back_rows = lax.psum(part_back.astype(jnp.bfloat16), "exp").astype(jnp.float32)
    gate_back = jnp.sum(back_rows * jax.nn.silu(pre_act), axis=1)
    slope_rows = (gate_col[:, None] * back_rows * silu_slope(pre_act)).astype(jnp.bfloat16)
    rows_grad = lax.dot_general(
        slope_rows, up_local, (((1,), (1,)), ((), ())), preferred_element_type=jnp.float32
    )
    rows_grad = rows_grad.astype(jnp.bfloat16).reshape(sources, item_count, share_width)
    gate_back = gate_back.astype(jnp.bfloat16).reshape(sources, item_count)
    grad_buffer = lax.all_to_all(rows_grad, "ctx", split_axis=0, concat_axis=0, tiled=True)
    gate_buffer = lax.all_to_all(gate_back, "ctx", split_axis=0, concat_axis=0, tiled=True)
    grad_flat = grad_buffer.reshape(experts * capacity, feature_share)
    input_grad = lax.dot_general(
        dispatch_rows, grad_flat, (((0,), (0,)), ((), ())), preferred_element_type=jnp.float32
    )
    gate_grad = jnp.einsum("jtk,j->tk", placed_float, gate_buffer.reshape(-1).astype(jnp.float32))
    return (input_grad.astype(jnp.bfloat16), gate_grad.astype(jnp.bfloat16))


def body(
    attn_query,
    attn_key,
    attn_value,
    log_decay,
    cotangent,
    expert_input,
    router_gates,
    expert_ids,
    up_weights,
    down_weights,
):
    query_grad, key_grad, value_grad = attention_part(
        attn_query, attn_key, attn_value, log_decay, cotangent
    )
    input_grad, gate_grad = expert_part(
        cotangent, expert_input, router_gates, expert_ids, up_weights, down_weights
    )
    return (query_grad, key_grad, value_grad, input_grad, gate_grad)


def solution(mesh):
    return jax.shard_map(
        body,
        mesh=mesh,
        in_specs=(
            P("ctx", "exp"),
            P("ctx", "exp"),
            P("ctx", "exp"),
            P("exp", "ctx"),
            P("ctx", "exp"),
            P("ctx", "exp"),
            P("ctx", None),
            P("ctx", None),
            P("ctx", "exp", None),
            P("ctx", None, "exp"),
        ),
        out_specs=(
            P("ctx", "exp"),
            P("ctx", "exp"),
            P("ctx", "exp"),
            P("ctx", "exp"),
            P("ctx", None),
        ),
        check_vma=False,
    )
```

profile of v0, /device:TPU:31, one launch (start us, length us, event | category | flops | bytes accessed | tf_op | source)
XLA Modules:
  0.0 465.7 jit_solution(6112903337878251845)
XLA Ops:
  11.6 3.4 convolution_convert_fusion.1
  15.0 6.4 %all-to-all-start.1 = ((bf16[16,40,2048]{2,1,0:T(8,128)(2,1)}), bf16[16,40,2048]{2,1,0:T(8,128)(2,1)S(1)}, u32[]{:S(2)}, u32[]{:S(2)}) async-start(bf16[16,40,2048]{2,1,0:T(8,128)(2,1)} %bitcast.22), calls=%async_computation.1 | async-start | bytes 5242880 | tf_op jit(solution)/shard_map/all_to_all | solution.py:134
  21.4 2.4 convolution_convert_fusion
  23.7 54.2 %all-to-all-done.1 = bf16[16,40,2048]{2,1,0:T(8,128)(2,1)S(1)} async-done(((bf16[16,40,2048]{2,1,0:T(8,128)(2,1)}), bf16[16,40,2048]{2,1,0:T(8,128)(2,1)S(1)}, u32[]{:S(2)}, u32[]{:S(2)}) %all-to-all-start.1) | async-done | bytes 2621472 | tf_op jit(solution)/shard_map/all_to_all | solution.py:134
  77.9 7.0 %all-to-all-start.2 = ((bf16[16,40,2048]{2,1,0:T(8,128)(2,1)}), bf16[16,40,2048]{2,1,0:T(8,128)(2,1)}, u32[]{:S(2)}, u32[]{:S(2)}) async-start(bf16[16,40,2048]{2,1,0:T(8,128)(2,1)} %bitcast.25), calls=%async_computation.2 | async-start | bytes 5242880 | tf_op jit(solution)/shard_map/all_to_all | solution.py:133
  85.0 8.3 %fusion.14 = bf16[640,1536]{1,0:T(8,128)(2,1)} fusion(bf16[640,2048]{1,0:T(8,128)(2,1)S(1)} %bitcast.160, bf16[1,1536,2048]{2,1,0:T(8,128)(2,1)} %param.23), kind=kOutput, calls=%fused_computation.23 | convolution fusion | flops 4027514880 | bytes 10878976 | tf_op jit(solution)/shard_map/dot_general | solution.py:141
  93.2 47.2 %all-to-all-done.2 = bf16[16,40,2048]{2,1,0:T(8,128)(2,1)} async-done(((bf16[16,40,2048]{2,1,0:T(8,128)(2,1)}), bf16[16,40,2048]{2,1,0:T(8,128)(2,1)}, u32[]{:S(2)}, u32[]{:S(2)}) %all-to-all-start.2) | async-done | bytes 2621472 | tf_op jit(solution)/shard_map/all_to_all | solution.py:133
  140.4 9.1 %fusion.17 = bf16[640,1536]{1,0:T(8,128)(2,1)} fusion(bf16[640,2048]{1,0:T(8,128)(2,1)} %bitcast.26, bf16[1,2048,1536]{2,1,0:T(8,128)(2,1)} %param.22), kind=kOutput, calls=%fused_computation.24 | convolution fusion | flops 4027514880 | bytes 10878976 | tf_op jit(solution)/shard_map/dot_general | solution.py:140
  155.0 9.3 %all_to_all.31 = bf16[16,1,40]{2,1,0:T(2,128)(2,1)S(1)} all-to-all(bf16[16,1,40]{2,1,0:T(2,128)(2,1)S(1)} %all_to_all.25), channel_id=1, replica_groups=mesh['ctx'=16,'exp'=2] {'ctx'}, dimensions={0} | all-to-all | bytes 2560 | tf_op jit(solution)/shard_map/all_to_all | solution.py:135
  164.4 14.2 %all-reduce.4.cloned.1.call-done = (bf16[640,1536]{1,0:T(8,128)(2,1)}, bf16[640,1536]{1,0:T(8,128)(2,1)}) async-done(((bf16[640,1536]{1,0:T(8,128)(2,1)}, bf16[640,1536]{1,0:T(8,128)(2,1)}), (bf16[640,1536]{1,0:T(8,128)(2,1)}, bf16[640,1536]{1,0:T(8,128)(2,1)})) %all-reduce.4.cloned.1.call-update) | async-done | bytes 3932176 | tf_op jit(solution)/shard_map/psum | solution.py:145
  178.6 3.4 fusion.8
  182.7 6.4 %all-to-all-start.4 = ((bf16[16,1,40]{2,1,0:T(2,128)(2,1)}), bf16[16,1,40]{2,1,0:T(2,128)(2,1)S(1)}, u32[]{:S(2)}, u32[]{:S(2)}) async-start(bf16[16,1,40]{2,1,0:T(2,128)(2,1)} %convert_element_type.212), calls=%async_computation.4 | async-start | bytes 16384 | tf_op jit(solution)/shard_map/all_to_all | solution.py:154
  189.1 10.5 %fusion.20 = bf16[640,2048]{1,0:T(8,128)(2,1)} fusion(bf16[1,2048,1536]{2,1,0:T(8,128)(2,1)} %param.22, bf16[640,1536]{1,0:T(8,128)(2,1)} %get-tuple-element.180, bf16[640,1536]{1,0:T(8,128)(2,1)} %get-tuple-element.181, f32[640]{0:T(1024)S(1)} %reshape.161), kind=kOutput, calls=%fused_computation.25 | convolution fusion | flops 4039639040 | bytes 12847616 | tf_op jit(solution)/shard_map/dot_general | solution.py:148
  199.6 6.4 %all-to-all-start.3 = ((bf16[16,40,2048]{2,1,0:T(8,128)(2,1)}), bf16[16,40,2048]{2,1,0:T(8,128)(2,1)S(1)}, u32[]{:S(2)}, u32[]{:S(2)}) async-start(bf16[16,40,2048]{2,1,0:T(8,128)(2,1)} %bitcast.159), calls=%async_computation.3 | async-start | bytes 5242880 | tf_op jit(solution)/shard_map/all_to_all | solution.py:153
  207.6 116.0 %all-reduce = bf16[256]{0:T(256)(128)(2,1)S(1)} all-reduce(bf16[256]{0:T(256)(128)(2,1)S(1)} %dynamic-update-slice), channel_id=2, replica_groups=mesh['ctx'=16,'exp'=2] {'ctx'}, use_global_device_ids=true, to_apply=%add | all-reduce | flops 256 | bytes 1024
  323.7 1.8 fusion.39
  326.3 1.5 convolution_bitcast_fusion.5
  328.7 1.4 convolution_convert_fusion.2
  331.3 1.6 fusion.31
  332.8 1.3 fusion.30
  334.2 93.8 %all-gather.6.cloned.1.call-done = bf16[256,128,128]{2,1,0:T(8,128)(2,1)} async-done(((bf16[16,128,128]{2,1,0:T(8,128)(2,1)}), bf16[256,128,128]{2,1,0:T(8,128)(2,1)}) %all-gather.6.cloned.1.call-update) | async-done | bytes 8388624 | tf_op jit(solution)/shard_map/all_gather | solution.py:12
  428.0 20.2 %while.26 = (s32[]{:T(128)}, f32[16,128,128]{2,1,0:T(8,128)S(1)}, s32[]{:T(128)}, bf16[16,16]{1,0:T(8,128)(2,1)S(1)}, bf16[16,16,128,128]{3,2,1,0:T(8,128)(2,1)}, /*index=5*/s32[]{:T(128)}, s32[]{:T(128)}, s32[]{:T(128)}) while((s32[]{:T(128)}, f32[16,128,128]{2,1,0:T(8,128)S(1)}, s32[]{:T(128)}, bf16[16,16]{1,0:T(8,128)(2,1)S(1)}, ...), condition=%wide.region_2.3_spmd, body=%wide.region_1.2_spmd.sunk | while | flops 786453 | bytes 2621735 | solution.py:27
  428.1 1.3 convert_add_fusion.4
  429.5 1.3 convert_add_fusion.4
  430.8 1.3 convert_add_fusion.4
  432.1 1.3 convert_add_fusion.4
  433.5 1.3 convert_add_fusion.4
  434.8 1.3 convert_add_fusion.4
  448.2 2.4 fusion.40
  450.6 2.1 copy.115
  452.7 1.5 fusion.37
  455.3 1.9 fusion.38
  (106 shorter events, 27.7 us)
Async XLA Ops:
  8.0 13.4 %copy-start = (bf16[128,2048]{1,0:T(8,128)(2,1)S(1)}, bf16[128,2048]{1,0:T(8,128)(2,1)}, u32[]{:S(2)}) copy-start(bf16[128,2048]{1,0:T(8,128)(2,1)} %param.19) | copy-start | bytes 1572868
  15.0 62.9 %all-to-all-start.1 = ((bf16[16,40,2048]{2,1,0:T(8,128)(2,1)}), bf16[16,40,2048]{2,1,0:T(8,128)(2,1)S(1)}, u32[]{:S(2)}, u32[]{:S(2)}) async-start(bf16[16,40,2048]{2,1,0:T(8,128)(2,1)} %bitcast.22), calls=%async_computation.1 | async-start | bytes 5242880 | tf_op jit(solution)/shard_map/all_to_all | solution.py:134
  77.9 62.5 %all-to-all-start.2 = ((bf16[16,40,2048]{2,1,0:T(8,128)(2,1)}), bf16[16,40,2048]{2,1,0:T(8,128)(2,1)}, u32[]{:S(2)}, u32[]{:S(2)}) async-start(bf16[16,40,2048]{2,1,0:T(8,128)(2,1)} %bitcast.25), calls=%async_computation.2 | async-start | bytes 5242880 | tf_op jit(solution)/shard_map/all_to_all | solution.py:133
  84.9 93.7 %all-reduce.4.cloned.1.call-start = ((), (), s32[]{:S(2)}) async-start(), calls=%async_computation.7 | async-start | bytes 7864320 | tf_op jit(solution)/shard_map/psum | solution.py:145
  149.5 1.0 copy-start.8
  149.5 1.3 copy-start.11
  149.5 1.6 copy-start.13
  149.6 3.5 copy-start.12
  149.6 3.8 copy-start.6
  149.6 4.9 %copy-start.14 = (bf16[128,4]{0,1:T(4,128)(2,1)S(1)}, bf16[128,4]{0,1:T(4,128)(2,1)}, u32[]{:S(2)}) copy-start(bf16[128,4]{0,1:T(4,128)(2,1)} %param.20) | copy-start | bytes 3076
  149.6 180.5 %all-gather.8.cloned.1.call-start = ((), (), s32[]{:S(2)}) async-start(), calls=%async_computation.6 | async-start | bytes 8912896 | tf_op jit(solution)/shard_map/all_gather | solution.py:12
  150.9 48.7 %copy-start.4 = (bf16[128,2048]{0,1:T(8,128)(2,1)}, bf16[128,2048]{0,1:T(8,128)(2,1)S(1)}, u32[]{:S(2)}) copy-start(bf16[128,2048]{0,1:T(8,128)(2,1)S(1)} %copy.124) | copy-start | bytes 1572868
  151.2 30.9 %copy-start.2 = (bf16[128,2048]{0,1:T(8,128)(2,1)}, bf16[128,2048]{0,1:T(8,128)(2,1)S(1)}, u32[]{:S(2)}) copy-start(bf16[128,2048]{0,1:T(8,128)(2,1)S(1)} %copy.101) | copy-start | bytes 1572868
  153.0 274.9 %all-gather.6.cloned.1.call-start = ((), (), s32[]{:S(2)}) async-start(), calls=%async_computation.5 | async-start | bytes 8912896 | tf_op jit(solution)/shard_map/all_gather | solution.py:12
  182.7 16.9 %all-to-all-start.4 = ((bf16[16,1,40]{2,1,0:T(2,128)(2,1)}), bf16[16,1,40]{2,1,0:T(2,128)(2,1)S(1)}, u32[]{:S(2)}, u32[]{:S(2)}) async-start(bf16[16,1,40]{2,1,0:T(2,128)(2,1)} %convert_element_type.212), calls=%async_computation.4 | async-start | bytes 16384 | tf_op jit(solution)/shard_map/all_to_all | solution.py:154
  199.6 6.4 %copy-start.15 = (u32[32]{0:T(128)S(1)}, u32[32]{0:T(128)}, u32[]{:S(2)}) copy-start(u32[32]{0:T(128)} %constant.80) | copy-start | bytes 388
  199.6 129.1 %all-to-all-start.3 = ((bf16[16,40,2048]{2,1,0:T(8,128)(2,1)}), bf16[16,40,2048]{2,1,0:T(8,128)(2,1)S(1)}, u32[]{:S(2)}, u32[]{:S(2)}) async-start(bf16[16,40,2048]{2,1,0:T(8,128)(2,1)} %bitcast.159), calls=%async_computation.3 | async-start | bytes 5242880 | tf_op jit(solution)/shard_map/all_to_all | solution.py:153
  325.5 0.8 copy-start.9
  330.2 1.0 copy-start.7
  428.0 20.2 %copy-start.5 = (bf16[128,2048]{0,1:T(8,128)(2,1)S(1)}, bf16[128,2048]{0,1:T(8,128)(2,1)}, u32[]{:S(2)}) copy-start(bf16[128,2048]{0,1:T(8,128)(2,1)} %copy-done.4) | copy-start | bytes 1572868
  448.2 4.5 copy-start.3
  448.2 4.5 copy-start.10
  450.6 7.6 %copy-start.1 = (bf16[128,2048]{1,0:T(8,128)(2,1)S(1)}, bf16[128,2048]{1,0:T(8,128)(2,1)}, u32[]{:S(2)}) copy-start(bf16[128,2048]{1,0:T(8,128)(2,1)} %param.19) | copy-start | bytes 1572868
Sparse Core Ops, SparseCore 0:
  149.7 28.8 all-reduce.3
Sparse Core Ops, SparseCore 1:
  153.4 160.4 all-gather.7
  317.1 110.8 all-gather.5
where the time goes:
time: 467 us; the launch traced here: 466 us
  waiting for transfers between devices  209 us (45%)
  blocking collectives  125 us (27%)
  matrix products  50 us (11%)
  other arithmetic  26.2 us (6%)
  starting transfers between devices  26.2 us (6%)
  between operations  16.4 us (4%)
  local copies, waits for them, and re-layouts  11.6 us (2%)
    unnamed x1, blocking collectives  116 us
    all_gather x2, waiting for transfers between devices, prefix(): lax.all_gather(a.astype(kind), axis)  93.8 us
    all_to_all x1, waiting for transfers between devices, expert_part(): lax.all_to_all(buffer_cot, 'ctx', split_axis=0, concat_axis=0, tiled=True)  54.2 us
    all_to_all x1, waiting for transfers between devices, expert_part(): lax.all_to_all(buffer_in, 'ctx', split_axis=0, concat_axis=0, tiled=True)  47.2 us
    add x15, other arithmetic, chain_step(): jnp.exp(later[0])[:, None, None] * earlier[1] + later[1]  19.5 us
    psum x1, waiting for transfers between devices, expert_part(): lax.psum(part_back.astype(jnp.bfloat16), 'exp').astype(jnp.float32)  14.2 us
    dot_general x1, matrix products, expert_part(): lax.dot_general(slope_rows, up_local, (((1,), (1,)), ((), ())), preferred...  10.5 us
  transfers between devices with their start and end apart: 7, of which 4 were waited for; matrix products, arithmetic and copies ran while one was open for 8% of the time, Pallas kernels for 0%

commit v1 on v0

--- a/solution.py
+++ b/solution.py
@@ -2,6 +2,22 @@
 import jax.numpy as jnp
 from jax import lax
 from jax.sharding import PartitionSpec as P
+
+
+def exchange_in_pairs(x, axis, split, join):
+    ways, here = (lax.axis_size(axis), lax.axis_index(axis))
+    width = x.shape[split] // ways
+    lengths = list(x.shape)
+    lengths[split] = width
+    height = lengths[join]
+    lengths[join] = height * ways
+    full = jnp.zeros(lengths, x.dtype)
+    for mask in range(ways):
+        part = lax.dynamic_slice_in_dim(x, (here ^ mask) * width, width, axis=split)
+        if mask:
+            part = lax.ppermute(part, axis, [(d, d ^ mask) for d in range(ways)])
+        full = lax.dynamic_update_slice_in_dim(full, part, (here ^ mask) * height, axis=join)
+    return full
 
 
 def prefix(value, axis, join, neutral, backward):
@@ -131,7 +147,7 @@
     up_local = up_weights[0]
     down_local = down_weights[0]
     inputs = lax.all_to_all(buffer_in, "ctx", split_axis=0, concat_axis=0, tiled=True)
-    cot_rows = lax.all_to_all(buffer_cot, "ctx", split_axis=0, concat_axis=0, tiled=True)
+    cot_rows = exchange_in_pairs(buffer_cot, "ctx", 0, 0)
     gate_rows = lax.all_to_all(buffer_gate, "ctx", split_axis=0, concat_axis=0, tiled=True)
     sources, item_count, share_width = inputs.shape
     flat_in = inputs.reshape(sources * item_count, share_width)

time: 467 us -> 468 us (level)
  waiting for transfers between devices: 209 us -> 174 us
  starting transfers between devices: 26.2 us -> 52.4 us
  blocking collectives: 125 us -> 140 us
  matrix products: 50 us -> 44.7 us
    ppermute x0 -> x15, waiting for transfers between devices: none -> 66.1 us  [exchange_in_pairs(): part = lax.ppermute(part, axis, [(d, d ^ mask) for d in range(ways)])]
    all_to_all x1 -> x0, waiting for transfers between devices: 54.2 us -> none  [expert_part(): lax.all_to_all(buffer_cot, 'ctx', split_axis=0, concat_axis=0, tiled=True)]
    all_to_all x1, waiting for transfers between devices: 47.2 us -> 0.01 us  [expert_part(): lax.all_to_all(buffer_in, 'ctx', split_axis=0, concat_axis=0, tiled=True)]
    ppermute x0 -> x15, starting transfers between devices: none -> 33 us  [exchange_in_pairs(): part = lax.ppermute(part, axis, [(d, d ^ mask) for d in range(ways)])]
    all_to_all x1, blocking collectives: 9.32 us -> 23.8 us  [expert_part(): lax.all_to_all(buffer_gate, 'ctx', split_axis=0, concat_axis=0, tiled=True)]
    all_to_all x1 -> x0, starting transfers between devices: 6.36 us -> none  [expert_part(): lax.all_to_all(buffer_cot, 'ctx', split_axis=0, concat_axis=0, tiled=True)]
  transfers between devices with their start and end apart: 7 -> 21, of which waited for: 4 -> 11; matrix products, arithmetic and copies ran while one was open for 8% -> 8% of each run, Pallas kernels for 0% -> 0%
where the time goes in v1:
time: 468 us; the launch traced here: 467 us
  waiting for transfers between devices  174 us (37%)
  blocking collectives  140 us (30%)
  starting transfers between devices  52.4 us (11%)
  matrix products  44.7 us (10%)
  other arithmetic  26.2 us (6%)
  between operations  16.8 us (4%)
  local copies, waits for them, and re-layouts  12.1 us (3%)
    unnamed x1, blocking collectives  116 us
    all_gather x2, waiting for transfers between devices, prefix(): lax.all_gather(a.astype(kind), axis)  93.8 us
    ppermute x15, waiting for transfers between devices, exchange_in_pairs(): part = lax.ppermute(part, axis, [(d, d ^ mask) for d in range(ways)])  66.1 us
    ppermute x15, starting transfers between devices, exchange_in_pairs(): part = lax.ppermute(part, axis, [(d, d ^ mask) for d in range(ways)])  33 us
    all_to_all x1, blocking collectives, expert_part(): lax.all_to_all(buffer_gate, 'ctx', split_axis=0, concat_axis=0, tiled=True)  23.8 us
    add x15, other arithmetic, chain_step(): jnp.exp(later[0])[:, None, None] * earlier[1] + later[1]  19.5 us
    psum x1, waiting for transfers between devices, expert_part(): lax.psum(part_back.astype(jnp.bfloat16), 'exp').astype(jnp.float32)  14.5 us
    dot_general x1, matrix products, expert_part(): lax.dot_general(slope_rows, up_local, (((1,), (1,)), ((), ())), preferred...  10.5 us
  transfers between devices with their start and end apart: 21, of which 11 were waited for; matrix products, arithmetic and copies ran while one was open for 8% of the time, Pallas kernels for 0%

profile of v1, /device:TPU:31, one launch (start us, length us, event | category | flops | bytes accessed | tf_op | source)
XLA Modules:
  0.0 466.9 jit_solution(11304046652859493189)
XLA Ops:
  11.6 2.4 convolution_convert_fusion
  14.0 6.5 %all-to-all-start.1 = ((bf16[16,40,2048]{2,1,0:T(8,128)(2,1)}), bf16[16,40,2048]{2,1,0:T(8,128)(2,1)}, u32[]{:S(2)}, u32[]{:S(2)}) async-start(bf16[16,40,2048]{2,1,0:T(8,128)(2,1)} %bitcast.25), calls=%async_computation.1 | async-start | bytes 5242880 | tf_op jit(solution)/shard_map/all_to_all | solution.py:149
  22.8 2.1 collective-permute-start.2
  26.4 11.0 %collective-permute-done = bf16[1,40,2048]{2,1,0:T(8,128)(2,1)S(1)} collective-permute-done((bf16[1,40,2048]{2,1,0:T(8,128)(2,1)S(1)}, bf16[1,40,2048]{2,1,0:T(8,128)(2,1)S(1)}, u32[]{:S(2)}, u32[]{:S(2)}) %collective-permute-start) | collective-permute-done | bytes 163872 | tf_op jit(solution)/shard_map/ppermute | solution.py:18
  37.4 7.7 %collective-permute-done.1 = bf16[1,40,2048]{2,1,0:T(8,128)(2,1)S(1)} collective-permute-done((bf16[1,40,2048]{2,1,0:T(8,128)(2,1)S(1)}, bf16[1,40,2048]{2,1,0:T(8,128)(2,1)S(1)}, u32[]{:S(2)}, u32[]{:S(2)}) %collective-permute-start.1) | collective-permute-done | bytes 163872 | tf_op jit(solution)/shard_map/ppermute | solution.py:18
  45.1 4.0 collective-permute-start.7
  49.1 17.2 %collective-permute-done.3 = bf16[1,40,2048]{2,1,0:T(8,128)(2,1)S(1)} collective-permute-done((bf16[1,40,2048]{2,1,0:T(8,128)(2,1)S(1)}, bf16[1,40,2048]{2,1,0:T(8,128)(2,1)S(1)}, u32[]{:S(2)}, u32[]{:S(2)}) %collective-permute-start.3) | collective-permute-done | bytes 163872 | tf_op jit(solution)/shard_map/ppermute | solution.py:18
  66.9 3.0 collective-permute-done.4
  71.2 2.2 collective-permute-done.5
  73.4 1.6 collective-permute-start.10
  75.0 1.9 collective-permute-done.6
  76.9 4.4 collective-permute-start.11
  81.3 17.7 %collective-permute-done.7 = bf16[1,40,2048]{2,1,0:T(8,128)(2,1)S(1)} collective-permute-done((bf16[1,40,2048]{2,1,0:T(8,128)(2,1)S(1)}, bf16[1,40,2048]{2,1,0:T(8,128)(2,1)S(1)}, u32[]{:S(2)}, u32[]{:S(2)}) %collective-permute-start.7) | collective-permute-done | bytes 163872 | tf_op jit(solution)/shard_map/ppermute | solution.py:18
  99.0 6.6 %collective-permute-start.12 = (bf16[1,40,2048]{2,1,0:T(8,128)(2,1)S(1)}, bf16[1,40,2048]{2,1,0:T(8,128)(2,1)S(1)}, u32[]{:S(2)}, u32[]{:S(2)}) collective-permute-start(bf16[1,40,2048]{2,1,0:T(8,128)(2,1)S(1)} %get-tuple-element.184), channel_id=1, source_target_pairs={{0,26},{2,24},{4,30},{6,28},{8,18},{10,16},{12,22},{14,20},{16,10}... | collective-permute-start | bytes 491528 | tf_op jit(solution)/shard_map/ppermute | solution.py:18
  105.8 2.7 collective-permute-done.9
  108.6 10.2 %collective-permute-start.14 = (bf16[1,40,2048]{2,1,0:T(8,128)(2,1)S(1)}, bf16[1,40,2048]{2,1,0:T(8,128)(2,1)S(1)}, u32[]{:S(2)}, u32[]{:S(2)}) collective-permute-start(bf16[1,40,2048]{2,1,0:T(8,128)(2,1)S(1)} %get-tuple-element.182), channel_id=1, source_target_pairs={{0,30},{2,28},{4,26},{6,24},{8,22},{10,20},{12,18},{14,16},{16,14}... | collective-permute-start | bytes 491528 | tf_op jit(solution)/shard_map/ppermute | solution.py:18
  118.9 2.6 collective-permute-done.14
  121.6 5.6 %fusion.14 = bf16[640,1536]{1,0:T(8,128)(2,1)} fusion(bf16[640,2048]{1,0:T(8,128)(2,1)S(1)} %bitcast.161, bf16[1,1536,2048]{2,1,0:T(8,128)(2,1)S(1)} %bitcast.169), kind=kOutput, calls=%fused_computation.23 | convolution fusion | flops 4027514880 | bytes 10878976 | tf_op jit(solution)/shard_map/dot_general | solution.py:157
  127.2 9.1 %fusion.17 = bf16[640,1536]{1,0:T(8,128)(2,1)} fusion(bf16[640,2048]{1,0:T(8,128)(2,1)} %bitcast.26, bf16[1,2048,1536]{2,1,0:T(8,128)(2,1)} %param.22), kind=kOutput, calls=%fused_computation.24 | convolution fusion | flops 4027514880 | bytes 10878976 | tf_op jit(solution)/shard_map/dot_general | solution.py:156
  141.4 23.8 %all_to_all.26 = bf16[16,1,40]{2,1,0:T(2,128)(2,1)S(1)} all-to-all(bf16[16,1,40]{2,1,0:T(2,128)(2,1)S(1)} %all_to_all.21), channel_id=1, replica_groups=mesh['ctx'=16,'exp'=2] {'ctx'}, dimensions={0} | all-to-all | bytes 2560 | tf_op jit(solution)/shard_map/all_to_all | solution.py:151
  165.4 14.5 %all-reduce.4.cloned.1.call-done = (bf16[640,1536]{1,0:T(8,128)(2,1)}, bf16[640,1536]{1,0:T(8,128)(2,1)}) async-done(((bf16[640,1536]{1,0:T(8,128)(2,1)}, bf16[640,1536]{1,0:T(8,128)(2,1)}), (bf16[640,1536]{1,0:T(8,128)(2,1)}, bf16[640,1536]{1,0:T(8,128)(2,1)})) %all-reduce.4.cloned.1.call-update) | async-done | bytes 3932176 | tf_op jit(solution)/shard_map/psum | solution.py:161
  179.8 3.4 fusion.8
  183.9 6.4 %all-to-all-start.3 = ((bf16[16,1,40]{2,1,0:T(2,128)(2,1)}), bf16[16,1,40]{2,1,0:T(2,128)(2,1)S(1)}, u32[]{:S(2)}, u32[]{:S(2)}) async-start(bf16[16,1,40]{2,1,0:T(2,128)(2,1)} %convert_element_type.212), calls=%async_computation.3 | async-start | bytes 16384 | tf_op jit(solution)/shard_map/all_to_all | solution.py:170
  190.3 10.5 %fusion.20 = bf16[640,2048]{1,0:T(8,128)(2,1)} fusion(bf16[1,2048,1536]{2,1,0:T(8,128)(2,1)} %param.22, bf16[640,1536]{1,0:T(8,128)(2,1)} %get-tuple-element.180, bf16[640,1536]{1,0:T(8,128)(2,1)} %get-tuple-element.181, f32[640]{0:T(1024)S(1)} %reshape.161), kind=kOutput, calls=%fused_computation.25 | convolution fusion | flops 4039639040 | bytes 12847616 | tf_op jit(solution)/shard_map/dot_general | solution.py:164
  200.8 6.5 %all-to-all-start.2 = ((bf16[16,40,2048]{2,1,0:T(8,128)(2,1)}), bf16[16,40,2048]{2,1,0:T(8,128)(2,1)S(1)}, u32[]{:S(2)}, u32[]{:S(2)}) async-start(bf16[16,40,2048]{2,1,0:T(8,128)(2,1)} %bitcast.160), calls=%async_computation.2 | async-start | bytes 5242880 | tf_op jit(solution)/shard_map/all_to_all | solution.py:169
  209.0 115.9 %all-reduce = bf16[256]{0:T(256)(128)(2,1)S(1)} all-reduce(bf16[256]{0:T(256)(128)(2,1)S(1)} %dynamic-update-slice), channel_id=2, replica_groups=mesh['ctx'=16,'exp'=2] {'ctx'}, use_global_device_ids=true, to_apply=%add | all-reduce | flops 256 | bytes 1024
  324.9 1.8 fusion.39
  335.3 93.8 %all-gather.6.cloned.1.call-done = bf16[256,128,128]{2,1,0:T(8,128)(2,1)} async-done(((bf16[16,128,128]{2,1,0:T(8,128)(2,1)}), bf16[256,128,128]{2,1,0:T(8,128)(2,1)}) %all-gather.6.cloned.1.call-update) | async-done | bytes 8388624 | tf_op jit(solution)/shard_map/all_gather | solution.py:28
  429.3 20.2 %while.26 = (s32[]{:T(128)}, f32[16,128,128]{2,1,0:T(8,128)S(1)}, s32[]{:T(128)}, bf16[16,16]{1,0:T(8,128)(2,1)S(1)}, bf16[16,16,128,128]{3,2,1,0:T(8,128)(2,1)}, /*index=5*/s32[]{:T(128)}, s32[]{:T(128)}, s32[]{:T(128)}) while((s32[]{:T(128)}, f32[16,128,128]{2,1,0:T(8,128)S(1)}, s32[]{:T(128)}, bf16[16,16]{1,0:T(8,128)(2,1)S(1)}, ...), condition=%wide.region_2.3_spmd, body=%wide.region_1.2_spmd.sunk | while | flops 786453 | bytes 2621735 | solution.py:43
  449.5 2.4 fusion.40
  451.9 2.0 copy.115
  456.5 1.9 fusion.38
  (156 shorter events, 48.3 us)
Async XLA Ops:
  8.0 3.6 copy-start
  14.0 6.6 %copy-start.8 = (bf16[128,2048]{1,0:T(8,128)(2,1)S(1)}, bf16[128,2048]{1,0:T(8,128)(2,1)}, u32[]{:S(2)}) copy-start(bf16[128,2048]{1,0:T(8,128)(2,1)} %param.18) | copy-start | bytes 1572868
  14.0 113.2 %all-to-all-start.1 = ((bf16[16,40,2048]{2,1,0:T(8,128)(2,1)}), bf16[16,40,2048]{2,1,0:T(8,128)(2,1)}, u32[]{:S(2)}, u32[]{:S(2)}) async-start(bf16[16,40,2048]{2,1,0:T(8,128)(2,1)} %bitcast.25), calls=%async_computation.1 | async-start | bytes 5242880 | tf_op jit(solution)/shard_map/all_to_all | solution.py:149
  20.5 159.3 %all-reduce.4.cloned.1.call-start = ((), (), s32[]{:S(2)}) async-start(), calls=%async_computation.6 | async-start | bytes 7864320 | tf_op jit(solution)/shard_map/psum | solution.py:161
  21.5 100.0 %slice-start = ((s8[6291456]{0:T(1024)(128)(4,1)}), s8[4194304]{0:T(1024)(128)(4,1)S(1)}, s32[]{:S(2)}) async-start(s8[6291456]{0:T(1024)(128)(4,1)} %bitcast.168), calls=%async_computation.7 | async-start | bytes 8388608
  21.9 99.7 %slice-start.1 = ((s8[6291456]{0:T(1024)(128)(4,1)}), s8[2097152]{0:T(1024)(128)(4,1)S(1)}, s32[]{:S(2)}) async-start(s8[6291456]{0:T(1024)(128)(4,1)} %bitcast.168), calls=%async_computation.8 | async-start | bytes 4194304
  22.2 15.2 %collective-permute-start = (bf16[1,40,2048]{2,1,0:T(8,128)(2,1)S(1)}, bf16[1,40,2048]{2,1,0:T(8,128)(2,1)S(1)}, u32[]{:S(2)}, u32[]{:S(2)}) collective-permute-start(bf16[1,40,2048]{2,1,0:T(8,128)(2,1)S(1)} %get-tuple-element.196), channel_id=1, source_target_pairs={{0,2},{2,0},{4,6},{6,4},{8,10},{10,8},{12,14},{14,12},{16,18},{18,... | collective-permute-start | bytes 491528 | tf_op jit(solution)/shard_map/ppermute | solution.py:18
  22.5 22.6 %collective-permute-start.1 = (bf16[1,40,2048]{2,1,0:T(8,128)(2,1)S(1)}, bf16[1,40,2048]{2,1,0:T(8,128)(2,1)S(1)}, u32[]{:S(2)}, u32[]{:S(2)}) collective-permute-start(bf16[1,40,2048]{2,1,0:T(8,128)(2,1)S(1)} %get-tuple-element.195), channel_id=1, source_target_pairs={{0,4},{2,6},{4,0},{6,2},{8,12},{10,14},{12,8},{14,10},{16,20},{18,... | collective-permute-start | bytes 491528 | tf_op jit(solution)/shard_map/ppermute | solution.py:18
  22.8 22.3 %collective-permute-start.2 = (bf16[1,40,2048]{2,1,0:T(8,128)(2,1)S(1)}, bf16[1,40,2048]{2,1,0:T(8,128)(2,1)S(1)}, u32[]{:S(2)}, u32[]{:S(2)}) collective-permute-start(bf16[1,40,2048]{2,1,0:T(8,128)(2,1)S(1)} %get-tuple-element.194), channel_id=1, source_target_pairs={{0,6},{2,4},{4,2},{6,0},{8,14},{10,12},{12,10},{14,8},{16,22},{18,... | collective-permute-start | bytes 491528 | tf_op jit(solution)/shard_map/ppermute | solution.py:18
  24.9 41.5 %collective-permute-start.3 = (bf16[1,40,2048]{2,1,0:T(8,128)(2,1)S(1)}, bf16[1,40,2048]{2,1,0:T(8,128)(2,1)S(1)}, u32[]{:S(2)}, u32[]{:S(2)}) collective-permute-start(bf16[1,40,2048]{2,1,0:T(8,128)(2,1)S(1)} %get-tuple-element.193), channel_id=1, source_target_pairs={{0,8},{2,10},{4,12},{6,14},{8,0},{10,2},{12,4},{14,6},{16,24},{18,... | collective-permute-start | bytes 491528 | tf_op jit(solution)/shard_map/ppermute | solution.py:18
  25.2 44.7 %collective-permute-start.4 = (bf16[1,40,2048]{2,1,0:T(8,128)(2,1)S(1)}, bf16[1,40,2048]{2,1,0:T(8,128)(2,1)S(1)}, u32[]{:S(2)}, u32[]{:S(2)}) collective-permute-start(bf16[1,40,2048]{2,1,0:T(8,128)(2,1)S(1)} %get-tuple-element.192), channel_id=1, source_target_pairs={{0,10},{2,8},{4,14},{6,12},{8,2},{10,0},{12,6},{14,4},{16,26},{18,... | collective-permute-start | bytes 491528 | tf_op jit(solution)/shard_map/ppermute | solution.py:18
  37.4 36.0 %collective-permute-start.5 = (bf16[1,40,2048]{2,1,0:T(8,128)(2,1)S(1)}, bf16[1,40,2048]{2,1,0:T(8,128)(2,1)S(1)}, u32[]{:S(2)}, u32[]{:S(2)}) collective-permute-start(bf16[1,40,2048]{2,1,0:T(8,128)(2,1)S(1)} %get-tuple-element.191), channel_id=1, source_target_pairs={{0,12},{2,14},{4,8},{6,10},{8,4},{10,6},{12,0},{14,2},{16,28},{18,... | collective-permute-start | bytes 491528 | tf_op jit(solution)/shard_map/ppermute | solution.py:18
  45.1 31.8 %collective-permute-start.6 = (bf16[1,40,2048]{2,1,0:T(8,128)(2,1)S(1)}, bf16[1,40,2048]{2,1,0:T(8,128)(2,1)S(1)}, u32[]{:S(2)}, u32[]{:S(2)}) collective-permute-start(bf16[1,40,2048]{2,1,0:T(8,128)(2,1)S(1)} %get-tuple-element.190), channel_id=1, source_target_pairs={{0,14},{2,12},{4,10},{6,8},{8,6},{10,4},{12,2},{14,0},{16,30},{18,... | collective-permute-start | bytes 491528 | tf_op jit(solution)/shard_map/ppermute | solution.py:18
  45.1 53.8 %collective-permute-start.7 = (bf16[1,40,2048]{2,1,0:T(8,128)(2,1)S(1)}, bf16[1,40,2048]{2,1,0:T(8,128)(2,1)S(1)}, u32[]{:S(2)}, u32[]{:S(2)}) collective-permute-start(bf16[1,40,2048]{2,1,0:T(8,128)(2,1)S(1)} %get-tuple-element.189), channel_id=1, source_target_pairs={{0,16},{2,18},{4,20},{6,22},{8,24},{10,26},{12,28},{14,30},{16,0},... | collective-permute-start | bytes 491528 | tf_op jit(solution)/shard_map/ppermute | solution.py:18
  66.4 39.2 %collective-permute-start.8 = (bf16[1,40,2048]{2,1,0:T(8,128)(2,1)S(1)}, bf16[1,40,2048]{2,1,0:T(8,128)(2,1)S(1)}, u32[]{:S(2)}, u32[]{:S(2)}) collective-permute-start(bf16[1,40,2048]{2,1,0:T(8,128)(2,1)S(1)} %get-tuple-element.188), channel_id=1, source_target_pairs={{0,18},{2,16},{4,22},{6,20},{8,26},{10,24},{12,30},{14,28},{16,2},... | collective-permute-start | bytes 491528 | tf_op jit(solution)/shard_map/ppermute | solution.py:18
  69.9 38.7 %collective-permute-start.9 = (bf16[1,40,2048]{2,1,0:T(8,128)(2,1)S(1)}, bf16[1,40,2048]{2,1,0:T(8,128)(2,1)S(1)}, u32[]{:S(2)}, u32[]{:S(2)}) collective-permute-start(bf16[1,40,2048]{2,1,0:T(8,128)(2,1)S(1)} %get-tuple-element.187), channel_id=1, source_target_pairs={{0,20},{2,22},{4,16},{6,18},{8,28},{10,30},{12,24},{14,26},{16,4},... | collective-permute-start | bytes 491528 | tf_op jit(solution)/shard_map/ppermute | solution.py:18
  73.4 45.4 %collective-permute-start.10 = (bf16[1,40,2048]{2,1,0:T(8,128)(2,1)S(1)}, bf16[1,40,2048]{2,1,0:T(8,128)(2,1)S(1)}, u32[]{:S(2)}, u32[]{:S(2)}) collective-permute-start(bf16[1,40,2048]{2,1,0:T(8,128)(2,1)S(1)} %get-tuple-element.186), channel_id=1, source_target_pairs={{0,22},{2,20},{4,18},{6,16},{8,30},{10,28},{12,26},{14,24},{16,6},... | collective-permute-start | bytes 491528 | tf_op jit(solution)/shard_map/ppermute | solution.py:18
  76.9 41.9 %collective-permute-start.11 = (bf16[1,40,2048]{2,1,0:T(8,128)(2,1)S(1)}, bf16[1,40,2048]{2,1,0:T(8,128)(2,1)S(1)}, u32[]{:S(2)}, u32[]{:S(2)}) collective-permute-start(bf16[1,40,2048]{2,1,0:T(8,128)(2,1)S(1)} %get-tuple-element.185), channel_id=1, source_target_pairs={{0,24},{2,26},{4,28},{6,30},{8,16},{10,18},{12,20},{14,22},{16,8},... | collective-permute-start | bytes 491528 | tf_op jit(solution)/shard_map/ppermute | solution.py:18
  99.0 19.8 %collective-permute-start.12 = (bf16[1,40,2048]{2,1,0:T(8,128)(2,1)S(1)}, bf16[1,40,2048]{2,1,0:T(8,128)(2,1)S(1)}, u32[]{:S(2)}, u32[]{:S(2)}) collective-permute-start(bf16[1,40,2048]{2,1,0:T(8,128)(2,1)S(1)} %get-tuple-element.184), channel_id=1, source_target_pairs={{0,26},{2,24},{4,30},{6,28},{8,18},{10,16},{12,22},{14,20},{16,10}... | collective-permute-start | bytes 491528 | tf_op jit(solution)/shard_map/ppermute | solution.py:18
  105.6 13.3 %collective-permute-start.13 = (bf16[1,40,2048]{2,1,0:T(8,128)(2,1)S(1)}, bf16[1,40,2048]{2,1,0:T(8,128)(2,1)S(1)}, u32[]{:S(2)}, u32[]{:S(2)}) collective-permute-start(bf16[1,40,2048]{2,1,0:T(8,128)(2,1)S(1)} %get-tuple-element.183), channel_id=1, source_target_pairs={{0,28},{2,30},{4,24},{6,26},{8,20},{10,22},{12,16},{14,18},{16,12}... | collective-permute-start | bytes 491528 | tf_op jit(solution)/shard_map/ppermute | solution.py:18
  108.6 13.0 %collective-permute-start.14 = (bf16[1,40,2048]{2,1,0:T(8,128)(2,1)S(1)}, bf16[1,40,2048]{2,1,0:T(8,128)(2,1)S(1)}, u32[]{:S(2)}, u32[]{:S(2)}) collective-permute-start(bf16[1,40,2048]{2,1,0:T(8,128)(2,1)S(1)} %get-tuple-element.182), channel_id=1, source_target_pairs={{0,30},{2,28},{4,26},{6,24},{8,22},{10,20},{12,18},{14,16},{16,14}... | collective-permute-start | bytes 491528 | tf_op jit(solution)/shard_map/ppermute | solution.py:18
  136.3 3.5 copy-start.6
  136.4 194.9 %all-gather.8.cloned.1.call-start = ((), (), s32[]{:S(2)}) async-start(), calls=%async_computation.5 | async-start | bytes 8912896 | tf_op jit(solution)/shard_map/all_gather | solution.py:28
  137.3 63.4 %copy-start.4 = (bf16[128,2048]{0,1:T(8,128)(2,1)}, bf16[128,2048]{0,1:T(8,128)(2,1)S(1)}, u32[]{:S(2)}) copy-start(bf16[128,2048]{0,1:T(8,128)(2,1)S(1)} %copy.124) | copy-start | bytes 1572868
  139.5 289.7 %all-gather.6.cloned.1.call-start = ((), (), s32[]{:S(2)}) async-start(), calls=%async_computation.4 | async-start | bytes 8912896 | tf_op jit(solution)/shard_map/all_gather | solution.py:28
  183.9 16.9 %all-to-all-start.3 = ((bf16[16,1,40]{2,1,0:T(2,128)(2,1)}), bf16[16,1,40]{2,1,0:T(2,128)(2,1)S(1)}, u32[]{:S(2)}, u32[]{:S(2)}) async-start(bf16[16,1,40]{2,1,0:T(2,128)(2,1)} %convert_element_type.212), calls=%async_computation.3 | async-start | bytes 16384 | tf_op jit(solution)/shard_map/all_to_all | solution.py:170
  200.8 6.5 %copy-start.15 = (u32[32]{0:T(128)S(1)}, u32[32]{0:T(128)}, u32[]{:S(2)}) copy-start(u32[32]{0:T(128)} %constant.112) | copy-start | bytes 388
  200.8 129.1 %all-to-all-start.2 = ((bf16[16,40,2048]{2,1,0:T(8,128)(2,1)}), bf16[16,40,2048]{2,1,0:T(8,128)(2,1)S(1)}, u32[]{:S(2)}, u32[]{:S(2)}) async-start(bf16[16,40,2048]{2,1,0:T(8,128)(2,1)} %bitcast.160), calls=%async_computation.2 | async-start | bytes 5242880 | tf_op jit(solution)/shard_map/all_to_all | solution.py:169
  429.3 20.2 %copy-start.5 = (bf16[128,2048]{0,1:T(8,128)(2,1)S(1)}, bf16[128,2048]{0,1:T(8,128)(2,1)}, u32[]{:S(2)}) copy-start(bf16[128,2048]{0,1:T(8,128)(2,1)} %copy-done.4) | copy-start | bytes 1572868
  449.4 4.5 copy-start.3
  449.5 4.5 copy-start.10
  455.5 4.0 copy-start.1
  (7 other events, 13.6 us)
Sparse Core Ops, SparseCore 0:
  136.5 43.3 all-reduce.3
Sparse Core Ops, SparseCore 1:
  140.2 174.8 all-gather.7
  318.3 110.8 all-gather.5
